TPU v7x, 32 devices: a whole 2x2x4 slice. The times are simulated.
32 devices in a mesh: fsdp: 4 (over y, core), ctx: 2 (over x), tp: 4 (over z).
Axes of the slice: x: 2, y: 2, z: 4, core: 2. Of those that a mesh axis runs over, the one named last changes fastest.
Arguments:
- inputs: bfloat16 [32, 320, 1024], P('fsdp', 'ctx'), may hold values from -6 to 6
- cotangent: bfloat16 [32, 320, 1024], P('fsdp', 'ctx'), may hold values from -6 to 6
- visible: int32 [32, 320], P('fsdp'), may hold values from 0 to 1, as said below
- w_qkv: float32 [1024, 3, 1024], P('fsdp', None, 'tp'), may hold values from -0.1875 to 0.1875
- b_qv: float32 [2, 1024], P(None, 'tp'), may hold values from -3 to 3
- w_out: float32 [1024, 1024], P('tp', 'fsdp'), may hold values from -0.75 to 0.75
- b_out: float32 [1024], replicated, may hold values from -3 to 3
- w_up: float32 [1024, 4096], P('fsdp', 'tp'), may hold values from -0.1875 to 0.1875
- b_up: float32 [4096], P('tp'), may hold values from -3 to 3
- w_down: float32 [4096, 1024], P('tp', 'fsdp'), may hold values from -0.09375 to 0.09375
- b_down: float32 [1024], replicated, may hold values from -3 to 3
- gain_one: float32 [1024], replicated, may hold values from 0.1 to 1.9
- shift_one: float32 [1024], replicated, may hold values from -3 to 3
- gain_two: float32 [1024], replicated, may hold values from 0.1 to 1.9
- shift_two: float32 [1024], replicated, may hold values from -3 to 3
Outputs:
- output: float32 [32, 320, 1024], P('fsdp', 'ctx')
- grad_inputs: float32 [32, 320, 1024], P('fsdp', 'ctx')
- grad_w_qkv: float32 [1024, 3, 1024], P('fsdp', None, 'tp')
- grad_b_qv: float32 [2, 1024], P(None, 'tp')
- grad_w_out: float32 [1024, 1024], P('tp', 'fsdp')
- grad_b_out: float32 [1024], replicated
- grad_w_up: float32 [1024, 4096], P('fsdp', 'tp')
- grad_b_up: float32 [4096], P('tp')
- grad_w_down: float32 [4096, 1024], P('tp', 'fsdp')
- grad_b_down: float32 [1024], replicated
- grad_gain_one: float32 [1024], replicated
- grad_shift_one: float32 [1024], replicated
- grad_gain_two: float32 [1024], replicated
- grad_shift_two: float32 [1024], replicated
Inputs may be any that keep to these rules, and one draw needn't show every extreme that they name: `visible`: the first 64 tokens of every image are 1; of the 256 image tokens of each image between a tenth and two fifths are 0.
All inputs are finite; a program needn't handle non-finite values.
Results may differ from a plain program's by a relative error of at most 0.012.
Values may be sent and summed in bfloat16 or wider, within the bound.
No kernel may reach another device: no remote copies, remote signals or barrier semaphores. Data moves between devices by JAX's collectives and lax.ppermute only.
A program may use at most 192 MiB of HBM per device.

v0:
```python
import jax
import jax.numpy as jnp
from jax import lax
from jax.sharding import PartitionSpec as P

HEAD = 64
EPSILON = 1e-06


def layer_norm(values, gain, shift):
    center = values - jnp.mean(values, axis=-1, keepdims=True)
    spread = jnp.mean(center * center, axis=-1, keepdims=True)
    return center * lax.rsqrt(spread + EPSILON) * gain + shift


def gelu_exact(values):
    return jax.nn.gelu(values, approximate=False)


def head_total(partial_sum):
    return lax.psum(partial_sum, "tp")


def attend(queries, keys_all, values_all, key_keep, scale_factor):
    scores = (
        jnp.einsum("iqhe,ikhe->ihqk", queries, keys_all, preferred_element_type=jnp.float32)
        * scale_factor
    )
    scores = jnp.where(key_keep, scores, -1e30)
    row_max = jnp.max(scores, axis=-1, keepdims=True)
    exponent = jnp.exp(scores - row_max)
    row_total = jnp.sum(exponent, axis=-1, keepdims=True)
    log_total = row_max + jnp.log(row_total)
    probability = exponent / row_total
    mixed = jnp.einsum(
        "ihqk,ikhe->iqhe",
        probability.astype(jnp.bfloat16),
        values_all,
        preferred_element_type=jnp.float32,
    )
    return (mixed, log_total)


def attend_back(queries, keys_all, values_all, key_keep, log_total, grad_mixed, scale_factor):
    again = (
        jnp.einsum("iqhe,ikhe->ihqk", queries, keys_all, preferred_element_type=jnp.float32)
        * scale_factor
    )
    again = jnp.where(key_keep, again, -1e30)
    prob_again = jnp.exp(again - log_total)
    grad_probs = jnp.einsum(
        "iqhe,ikhe->ihqk", grad_mixed, values_all, preferred_element_type=jnp.float32
    )
    grad_values = jnp.einsum(
        "ihqk,iqhe->ikhe",
        prob_again.astype(jnp.bfloat16),
        grad_mixed,
        preferred_element_type=jnp.float32,
    )
    grad_scores = prob_again * (
        grad_probs - jnp.sum(grad_probs * prob_again, axis=-1, keepdims=True)
    )
    grad_scores_low = grad_scores.astype(jnp.bfloat16)
    grad_queries = (
        jnp.einsum("ihqk,ikhe->iqhe", grad_scores_low, keys_all, preferred_element_type=jnp.float32)
        * scale_factor
    )
    grad_keys = (
        jnp.einsum("ihqk,iqhe->ikhe", grad_scores_low, queries, preferred_element_type=jnp.float32)
        * scale_factor
    )
    return (grad_queries, grad_keys, grad_values)


def on_device(
    inputs,
    cotangent,
    visible,
    w_qkv,
    b_qv,
    w_out,
    b_out,
    w_up,
    b_up,
    w_down,
    b_down,
    gain_one,
    shift_one,
    gain_two,
    shift_two,
):
    images, row_count, model_width = inputs.shape
    seq_total = visible.shape[1]
    tokens = images * row_count
    scale_factor = HEAD ** (-0.5)
    first_row = lax.axis_index("ctx") * row_count
    row_keep = (
        lax.dynamic_slice_in_dim(visible, first_row, row_count, 1)
        .astype(jnp.float32)
        .reshape(tokens, 1)
    )
    key_keep = (visible > 0)[:, None, None, :]
    qkv_w, out_w, up_w, down_w = (
        lax.all_gather(w_qkv.astype(jnp.bfloat16), "fsdp", axis=0, tiled=True),
        lax.all_gather(w_out.astype(jnp.bfloat16), "fsdp", axis=1, tiled=True),
        lax.all_gather(w_up.astype(jnp.bfloat16), "fsdp", axis=0, tiled=True),
        lax.all_gather(w_down.astype(jnp.bfloat16), "fsdp", axis=1, tiled=True),
    )
    local_width = qkv_w.shape[2]
    local_heads = local_width // HEAD
    flat_in = inputs.astype(jnp.float32).reshape(tokens, model_width)
    normed, norm_one_back = jax.vjp(layer_norm, flat_in, gain_one, shift_one)
    normed_low = normed.astype(jnp.bfloat16)
    bias_all = jnp.stack([b_qv[0], jnp.zeros_like(b_qv[0]), b_qv[1]])
    projected = (
        jnp.einsum("td,dcf->tcf", normed_low, qkv_w, preferred_element_type=jnp.float32) + bias_all
    )
    projected_low = projected.astype(jnp.bfloat16)
    queries = projected_low[:, 0].reshape(images, row_count, local_heads, HEAD)
    keys_here = projected_low[:, 1].reshape(images, row_count, local_width)
    values_here = projected_low[:, 2].reshape(images, row_count, local_width)
    keys_all, values_all = (
        lax.all_gather(keys_here, "ctx", axis=1, tiled=True),
        lax.all_gather(values_here, "ctx", axis=1, tiled=True),
    )
    keys_all = keys_all.reshape(images, seq_total, local_heads, HEAD)
    values_all = values_all.reshape(images, seq_total, local_heads, HEAD)
    mixed_heads, log_total = attend(queries, keys_all, values_all, key_keep, scale_factor)
    mixed_low = mixed_heads.astype(jnp.bfloat16).reshape(tokens, local_width)
    attended = head_total(jnp.dot(mixed_low, out_w, preferred_element_type=jnp.float32)) + b_out
    residual = flat_in + attended
    normed_two, norm_two_back = jax.vjp(layer_norm, residual, gain_two, shift_two)
    normed_two_low = normed_two.astype(jnp.bfloat16)
    hidden = jnp.dot(normed_two_low, up_w, preferred_element_type=jnp.float32) + b_up
    active, gelu_back = jax.vjp(gelu_exact, hidden)
    active_low = active.astype(jnp.bfloat16)
    branch = head_total(jnp.dot(active_low, down_w, preferred_element_type=jnp.float32)) + b_down
    result = row_keep * (residual + branch)
    grad_out = cotangent.astype(jnp.float32).reshape(tokens, model_width) * row_keep
    grad_branch = grad_out.astype(jnp.bfloat16)
    down_grad = jnp.dot(active_low.T, grad_branch, preferred_element_type=jnp.float32)
    down_bias_grad = jnp.sum(grad_branch.astype(jnp.float32), axis=0)
    grad_active = jnp.dot(grad_branch, down_w.T, preferred_element_type=jnp.float32)
    (grad_hidden,) = gelu_back(grad_active)
    grad_hidden_low = grad_hidden.astype(jnp.bfloat16)
    up_bias_grad = jnp.sum(grad_hidden_low.astype(jnp.float32), axis=0)
    up_grad = jnp.dot(normed_two_low.T, grad_hidden_low, preferred_element_type=jnp.float32)
    grad_normed_two = head_total(
        jnp.dot(grad_hidden_low, up_w.T, preferred_element_type=jnp.float32)
    )
    grad_resid_norm, gain_two_grad, shift_two_grad = norm_two_back(grad_normed_two)
    grad_resid = grad_out + grad_resid_norm
    grad_attended = grad_resid.astype(jnp.bfloat16)
    out_bias_grad = jnp.sum(grad_attended.astype(jnp.float32), axis=0)
    out_grad = jnp.dot(mixed_low.T, grad_attended, preferred_element_type=jnp.float32)
    grad_mixed_low = jnp.dot(grad_attended, out_w.T, preferred_element_type=jnp.float32).astype(
        jnp.bfloat16
    )
    grad_mixed = grad_mixed_low.reshape(images, row_count, local_heads, HEAD)
    grad_queries, grad_keys, grad_values = attend_back(
        queries, keys_all, values_all, key_keep, log_total, grad_mixed, scale_factor
    )
    grad_keys_here, grad_values_here = (
        lax.psum_scatter(
            grad_keys.reshape(images, seq_total, local_width),
            "ctx",
            scatter_dimension=1,
            tiled=True,
        ),
        lax.psum_scatter(
            grad_values.reshape(images, seq_total, local_width),
            "ctx",
            scatter_dimension=1,
            tiled=True,
        ),
    )
    grad_projected = jnp.stack(
        [
            grad_queries.reshape(tokens, local_width),
            grad_keys_here.reshape(tokens, local_width),
            grad_values_here.reshape(tokens, local_width),
        ],
        axis=1,
    ).astype(jnp.bfloat16)
    qv_bias_grad = jnp.sum(grad_projected.astype(jnp.float32)[:, 0::2], axis=0)
    qkv_grad = jnp.einsum(
        "td,tcf->dcf", normed_low, grad_projected, preferred_element_type=jnp.float32
    )
    grad_normed = head_total(
        jnp.einsum("tcf,dcf->td", grad_projected, qkv_w, preferred_element_type=jnp.float32)
    )
    grad_input_norm, gain_one_grad, shift_one_grad = norm_one_back(grad_normed)
    grad_input = (grad_resid + grad_input_norm).reshape(images, row_count, model_width)
    spread = (
        lax.psum_scatter(qkv_grad, "fsdp", scatter_dimension=0, tiled=True),
        lax.psum_scatter(out_grad, "fsdp", scatter_dimension=1, tiled=True),
        lax.psum_scatter(up_grad, "fsdp", scatter_dimension=0, tiled=True),
        lax.psum_scatter(down_grad, "fsdp", scatter_dimension=1, tiled=True),
    )
    qkv_total, out_total, up_total, down_total = lax.psum(
        (spread[0], spread[1], spread[2], spread[3]), "ctx"
    )
    small = lax.psum(
        (
            qv_bias_grad,
            out_bias_grad,
            up_bias_grad,
            down_bias_grad,
            gain_one_grad,
            shift_one_grad,
            gain_two_grad,
            shift_two_grad,
        ),
        ("fsdp", "ctx"),
    )
    return (
        result.reshape(images, row_count, model_width),
        grad_input,
        qkv_total,
        small[0],
        out_total,
        small[1],
        up_total,
        small[2],
        down_total,
        small[3],
        small[4],
        small[5],
        small[6],
        small[7],
    )


def solution(mesh):
    placed = (
        P("fsdp", "ctx", None),
        P("fsdp", "ctx", None),
        P("fsdp", None),
        P("fsdp", None, "tp"),
        P(None, "tp"),
        P("tp", "fsdp"),
        P(),
        P("fsdp", "tp"),
        P("tp"),
        P("tp", "fsdp"),
        P(),
        P(),
        P(),
        P(),
        P(),
    )
    return jax.shard_map(
        on_device,
        mesh=mesh,
        in_specs=placed,
        out_specs=(
            P("fsdp", "ctx", None),
            P("fsdp", "ctx", None),
            P("fsdp", None, "tp"),
            P(None, "tp"),
            P("tp", "fsdp"),
            P(),
            P("fsdp", "tp"),
            P("tp"),
            P("tp", "fsdp"),
            P(),
            P(),
            P(),
            P(),
            P(),
        ),
        check_vma=False,
    )
```

profile of v0, /device:TPU:0, one launch (start us, length us, event | category | flops | bytes accessed | tf_op | source)
XLA Modules:
  0.0 1293.8 jit_solution(9456932758075033936)
XLA Ops:
  15.6 17.0 %all-gather.6.cloned.1.call-done = bf16[1024,3,256]{2,0,1:T(8,128)(2,1)} async-done(((bf16[256,3,256]{2,0,1:T(8,128)(2,1)}), bf16[1024,3,256]{2,0,1:T(8,128)(2,1)}) %all-gather.6.cloned.1.call-update) | async-done | bytes 1572880 | tf_op jit(solution)/shard_map/all_gather | solution.py:104
  38.3 7.6 all_gather.21
  51.2 11.4 all-gather.10.cloned.1.call-done
  74.6 14.4 %all-gather.8.cloned.1.call-done = bf16[8,320,256]{2,1,0:T(8,128)(2,1)} async-done(((bf16[8,160,256]{2,1,0:T(8,128)(2,1)}), bf16[8,320,256]{2,1,0:T(8,128)(2,1)}) %all-gather.8.cloned.1.call-update) | async-done | bytes 1310736 | tf_op jit(solution)/shard_map/all_gather | solution.py:124
  91.6 5.1 fusion.30
  109.5 4.5 fusion.19
  114.0 179.8 %all-reduce.8.cloned.1.call-done = f32[1280,1024]{1,0:T(8,128)} async-done(((f32[1280,1024]{1,0:T(8,128)}), f32[1280,1024]{1,0:T(8,128)}) %all-reduce.8.cloned.1.call-update) | async-done | bytes 5242896 | tf_op jit(solution)/shard_map/psum | solution.py:21
  300.1 17.3 %all-gather.12.cloned.1.call-done = bf16[1024,1024]{1,0:T(8,128)(2,1)} async-done(((bf16[256,1024]{1,0:T(8,128)(2,1)}), bf16[1024,1024]{1,0:T(8,128)(2,1)}) %all-gather.12.cloned.1.call-update) | async-done | bytes 2097168 | tf_op jit(solution)/shard_map/all_gather | solution.py:106
  317.4 8.5 fusion.39
  325.9 16.3 %all-gather.14.cloned.1.call-done = bf16[1024,1024]{1,0:T(8,128)(2,1)} async-done(((bf16[1024,256]{1,0:T(8,128)(2,1)}), bf16[1024,1024]{1,0:T(8,128)(2,1)}) %all-gather.14.cloned.1.call-update) | async-done | bytes 2097168 | tf_op jit(solution)/shard_map/all_gather | solution.py:107
  342.3 18.4 %convert_reduce_fusion.2 = (f32[1024]{0:T(1024)S(1)}, bf16[1280,1024]{1,0:T(8,128)(2,1)S(1)}, f32[1280,1024]{1,0:T(8,128)}) fusion(f32[1280,1024]{1,0:T(8,128)} %fusion.39, f32[1024]{0:T(1024)S(1)} %copy-done.29, bf16[1280,1024]{1,0:T(8,128)(2,1)} %fusion.19, bf16[1024,1024]{1,0:T(8,128)(2,1)} %all-gather.14.cloned.1.call-done), kind=kOutput, calls=%fused_computation.31 | convolution fusion | flops 2782657536 | bytes 17833984 | tf_op jit(solution)/shard_map/dot_general | solution.py:143
  362.1 4.7 fusion.49
  367.3 188.6 %all-reduce.10.cloned.1.call-done = f32[1280,1024]{1,0:T(8,128)} async-done(((f32[1280,1024]{1,0:T(8,128)}), f32[1280,1024]{1,0:T(8,128)}) %all-reduce.10.cloned.1.call-update) | async-done | bytes 5242896 | tf_op jit(solution)/shard_map/psum | solution.py:21
  555.9 5.2 multiply_reduce_fusion.1
  577.5 7.2 fusion.20
  588.4 7.3 multiply_reduce_fusion
  595.8 5.4 multiply_convert_fusion
  611.4 5.6 multiply_convert_fusion.2
  618.5 4.5 fusion.51
  623.1 8.6 fusion.38
  632.0 6.2 fusion.31
  646.2 18.7 %reduce-scatter.7.cloned.1.call-done = f32[8,160,256]{2,0,1:T(8,128)} async-done(((f32[8,320,256]{2,0,1:T(8,128)}), f32[8,160,256]{2,0,1:T(8,128)}) %reduce-scatter.7.cloned.1.call-update) | async-done | bytes 1310736 | tf_op jit(solution)/shard_map/reduce_scatter | solution.py:164
  667.3 5.8 fusion.26
  673.2 8.0 fusion.48
  681.2 4.6 convolution_bitcast_fusion
  692.8 47.2 %reduce-scatter.17.cloned.1.call-done = f32[1024,256]{1,0:T(8,128)} async-done(((f32[1024,1024]{1,0:T(8,128)}), f32[1024,256]{1,0:T(8,128)}) %reduce-scatter.17.cloned.1.call-update) | async-done | bytes 1048592 | tf_op jit(solution)/shard_map/reduce_scatter | solution.py:198
  740.0 46.9 %reduce-scatter.15.cloned.1.call-done = f32[256,1024]{1,0:T(8,128)} async-done(((f32[1024,1024]{1,0:T(8,128)}), f32[256,1024]{1,0:T(8,128)}) %reduce-scatter.15.cloned.1.call-update) | async-done | bytes 1048592 | tf_op jit(solution)/shard_map/reduce_scatter | solution.py:197
  787.0 40.7 %reduce-scatter.11.cloned.1.call-done = f32[256,3,256]{2,0,1:T(8,128)} async-done(((f32[1024,3,256]{2,0,1:T(8,128)}), f32[256,3,256]{2,0,1:T(8,128)}) %reduce-scatter.11.cloned.1.call-update) | async-done | bytes 786448 | tf_op jit(solution)/shard_map/reduce_scatter | solution.py:195
  827.7 362.2 %all-reduce.12.cloned.1.call-done = (f32[1280,1024]{1,0:T(8,128)}, f32[1280,1024]{1,0:T(8,128)}) async-done(((f32[1280,1024]{1,0:T(8,128)}, f32[1280,1024]{1,0:T(8,128)}), (f32[1280,1024]{1,0:T(8,128)}, f32[1280,1024]{1,0:T(8,128)})) %all-reduce.12.cloned.1.call-update) | async-done | bytes 10485776 | tf_op jit(solution)/shard_map/psum | solution.py:21
  1196.9 25.6 %all-reduce = (f32[2,256]{1,0:T(2,128)}, f32[1024]{0:T(1024)}, f32[1024]{0:T(1024)}, f32[1024]{0:T(1024)}, f32[1024]{0:T(1024)}, /*index=5*/f32[1024]{0:T(1024)}, f32[1024]{0:T(1024)}, f32[1024]{0:T(1024)}) all-reduce(f32[2,256]{1,0:T(2,128)S(1)} %convert_reduce_fusion.4, ...), channel_id=1, replica_groups=mesh['fsdp'=4,'ctx'=2,'tp'=4] {'fsdp','ctx'}, use_global_device_ids=true, to_apply=%region_20.21 | all-reduce | flops 7680 | bytes 61440 | tf_op jit(solution)/shard_map/psum | solution.py:203
  1222.5 13.8 %add_add_fusion.2 = (f32[1280,1024]{1,0:T(8,128)}, f32[1280,1024]{1,0:T(8,128)}) fusion(f32[1280,1024]{1,0:T(8,128)} %copy-done.4, bf16[8,160,1024]{2,1,0:T(8,128)(2,1)} %param.16, f32[1280]{0:T(1024)S(1)} %negate_multiply_fusion.1, f32[1280]{0:T(1024)S(1)} %negate_multiply_fusion.2, f32[1280]{0:T(1024)S(1)} %mul.190, f32[1280]{0:T(1024)S(1)} %multiply_multiply_fusion.5, ...), kind=kLoop, calls=%fused_computation.33 | loop fusion | flops 20971520 | bytes 36739072 | tf_op jit(solution)/shard_map/add | solution.py:193
  1236.3 42.5 %all-reduce.14.cloned.1.call-done = (f32[256,3,256]{2,0,1:T(8,128)}, f32[256,256]{1,0:T(8,128)}, f32[256,1024]{1,0:T(8,128)}, f32[1024,256]{1,0:T(8,128)}) async-done(((f32[256,3,256]{2,0,1:T(8,128)}, f32[256,256]{1,0:T(8,128)}, f32[256,1024]{1,0:T(8,128)}, f32[1024,256]{1,0:T(8,128)}), (f32[256,3,256]{2,0,1:T(8,128)}, f32[256,256]{1,0:T(8,128)}, f32[256,1024]{1,0:T(8,128)}, ...) | async-done | bytes 3145744 | tf_op jit(solution)/shard_map/psum | solution.py:200
  (166 shorter events, 119.3 us)
Async XLA Ops:
  7.2 25.4 %all-gather.6.cloned.1.call-start = ((), (), s32[]{:S(2)}) async-start(), calls=%async_computation.6 | async-start | bytes 1966080 | tf_op jit(solution)/shard_map/all_gather | solution.py:104
  9.4 53.3 %all-gather.10.cloned.1.call-start = ((), (), s32[]{:S(2)}) async-start(), calls=%async_computation.8 | async-start | bytes 1966080 | tf_op jit(solution)/shard_map/all_gather | solution.py:123
  11.7 20.9 %copy-start.17 = (f32[1280]{0:T(1024)}, f32[1280]{0:T(1024)S(1)}, u32[]{:S(2)}) copy-start(f32[1280]{0:T(1024)S(1)} %div.47) | copy-start | bytes 15364
  12.6 20.0 %copy-start.21 = (f32[1280]{0:T(1024)}, f32[1280]{0:T(1024)S(1)}, u32[]{:S(2)}) copy-start(f32[1280]{0:T(1024)S(1)} %add.140) | copy-start | bytes 15364
  15.6 22.7 %copy-start.16 = (f32[256,256]{1,0:T(8,128)S(1)}, f32[256,256]{1,0:T(8,128)}, u32[]{:S(2)}) copy-start(f32[256,256]{1,0:T(8,128)} %param.20) | copy-start | bytes 786436
  37.0 9.2 copy-start.25
  38.2 50.8 %all-gather.8.cloned.1.call-start = ((), (), s32[]{:S(2)}) async-start(), calls=%async_computation.7 | async-start | bytes 1966080 | tf_op jit(solution)/shard_map/all_gather | solution.py:124
  46.0 247.8 %all-reduce.8.cloned.1.call-start = ((), (), s32[]{:S(2)}) async-start(), calls=%async_computation.9 | async-start | bytes 10485760 | tf_op jit(solution)/shard_map/psum | solution.py:21
  104.7 189.1 %copy-start.28 = (f32[1024]{0:T(1024)S(1)}, f32[1024]{0:T(1024)}, u32[]{:S(2)}) copy-start(f32[1024]{0:T(1024)} %param.21) | copy-start | bytes 12292
  104.8 212.6 %all-gather.12.cloned.1.call-start = ((), (), s32[]{:S(2)}) async-start(), calls=%async_computation.10 | async-start | bytes 2621440 | tf_op jit(solution)/shard_map/all_gather | solution.py:106
  106.9 235.3 %all-gather.14.cloned.1.call-start = ((), (), s32[]{:S(2)}) async-start(), calls=%async_computation.11 | async-start | bytes 2621440 | tf_op jit(solution)/shard_map/all_gather | solution.py:107
  109.1 446.8 %all-reduce.10.cloned.1.call-start = ((), (), s32[]{:S(2)}) async-start(), calls=%async_computation.12 | async-start | bytes 10485760 | tf_op jit(solution)/shard_map/psum | solution.py:21
  297.1 20.3 %copy-start.26 = (f32[1024]{0:T(1024)S(1)}, f32[1024]{0:T(1024)}, u32[]{:S(2)}) copy-start(f32[1024]{0:T(1024)} %param.28) | copy-start | bytes 12292
  297.1 20.3 %copy-start.34 = (f32[1024]{0:T(1024)S(1)}, f32[1024]{0:T(1024)}, u32[]{:S(2)}) copy-start(f32[1024]{0:T(1024)} %param.29) | copy-start | bytes 12292
  300.1 42.2 %copy-start.29 = (f32[1024]{0:T(1024)S(1)}, f32[1024]{0:T(1024)}, u32[]{:S(2)}) copy-start(f32[1024]{0:T(1024)} %param.23) | copy-start | bytes 12292
  342.3 19.8 %copy-start.32 = (bf16[1024,1024]{1,0:T(8,128)(2,1)S(1)}, bf16[1024,1024]{1,0:T(8,128)(2,1)}, u32[]{:S(2)}) copy-start(bf16[1024,1024]{1,0:T(8,128)(2,1)} %all-gather.12.cloned.1.call-done) | copy-start | bytes 6291460
  366.8 277.9 %reduce-scatter.9.cloned.1.call-start = ((), (), s32[]{:S(2)}) async-start(), calls=%async_computation.14 | async-start | bytes 3932160 | tf_op jit(solution)/shard_map/reduce_scatter | solution.py:170
  588.2 76.7 %reduce-scatter.7.cloned.1.call-start = ((), (), s32[]{:S(2)}) async-start(), calls=%async_computation.13 | async-start | bytes 3932160 | tf_op jit(solution)/shard_map/reduce_scatter | solution.py:164
  607.7 85.1 %reduce-scatter.13.cloned.1.call-start = ((), (), s32[]{:S(2)}) async-start(), calls=%async_computation.16 | async-start | bytes 1310720 | tf_op jit(solution)/shard_map/reduce_scatter | solution.py:196
  611.3 128.7 %reduce-scatter.17.cloned.1.call-start = ((), (), s32[]{:S(2)}) async-start(), calls=%async_computation.18 | async-start | bytes 5242880 | tf_op jit(solution)/shard_map/reduce_scatter | solution.py:198
  623.1 163.9 %reduce-scatter.15.cloned.1.call-start = ((), (), s32[]{:S(2)}) async-start(), calls=%async_computation.17 | async-start | bytes 5242880 | tf_op jit(solution)/shard_map/reduce_scatter | solution.py:197
  631.8 195.9 %reduce-scatter.11.cloned.1.call-start = ((), (), s32[]{:S(2)}) async-start(), calls=%async_computation.15 | async-start | bytes 3932160 | tf_op jit(solution)/shard_map/reduce_scatter | solution.py:195
  673.1 516.7 %all-reduce.12.cloned.1.call-start = ((), (), s32[]{:S(2)}) async-start(), calls=%async_computation.19 | async-start | bytes 20971520 | tf_op jit(solution)/shard_map/psum | solution.py:21
  673.2 8.0 copy-start.13
  673.2 8.0 copy-start.14
  673.2 8.0 copy-start.33
  685.8 504.1 %copy-start.18 = (f32[1280]{0:T(1024)S(1)}, f32[1280]{0:T(1024)}, u32[]{:S(2)}) copy-start(f32[1280]{0:T(1024)} %copy-done.17) | copy-start | bytes 15364
  685.8 504.1 %copy-start.24 = (f32[1024]{0:T(1024)S(1)}, f32[1024]{0:T(1024)}, u32[]{:S(2)}) copy-start(f32[1024]{0:T(1024)} %param.26) | copy-start | bytes 12292
  685.8 592.9 %all-reduce.14.cloned.1.call-start = ((), (), s32[]{:S(2)}) async-start(), calls=%async_computation.20 | async-start | bytes 6291456 | tf_op jit(solution)/shard_map/psum | solution.py:200
  827.6 366.1 %copy-start.22 = (f32[1280]{0:T(1024)S(1)}, f32[1280]{0:T(1024)}, u32[]{:S(2)}) copy-start(f32[1280]{0:T(1024)} %copy-done.21) | copy-start | bytes 15364
  827.6 366.1 %copy-start.20 = (f32[1280]{0:T(1024)S(1)}, f32[1280]{0:T(1024)}, u32[]{:S(2)}) copy-start(f32[1280]{0:T(1024)} %copy-done.19) | copy-start | bytes 15364
  1193.7 28.8 %copy-start.30 = (f32[1024]{0:T(1024)S(1)}, f32[1024]{0:T(1024)}, u32[]{:S(2)}) copy-start(f32[1024]{0:T(1024)} %param.25) | copy-start | bytes 12292
  (19 other events, 69.1 us)
Sparse Core Ops, SparseCore 0:
  10.2 22.3 all-gather.5
  38.3 24.2 all-gather.9
  64.7 24.2 all-gather.7
  104.9 188.8 all-reduce.7
  295.8 21.5 all-gather.11
  319.4 22.8 all-gather.13
  366.9 188.9 all-reduce.9
  588.3 36.5 reduce-scatter.8
  627.3 37.5 reduce-scatter.6
  667.8 24.8 reduce-scatter.12
  695.5 44.5 reduce-scatter.16
  742.4 44.5 reduce-scatter.14
  789.7 37.9 reduce-scatter.10
  830.7 359.1 all-reduce.11
  1192.2 86.5 all-reduce.13
where the time goes:
time: 1300 us; the launch traced here: 1290 us
  waiting for transfers between devices  1010 us (78%)
  matrix products  110 us (8%)
  other arithmetic  71.5 us (6%)
  local copies, waits for them, and re-layouts  56.8 us (4%)
  blocking collectives  33.2 us (3%)
  between operations  14.7 us (1%)
    psum x3, waiting for transfers between devices, head_total(): return lax.psum(partial_sum, 'tp')  731 us
    reduce_scatter x1, waiting for transfers between devices, on_device(): lax.psum_scatter(down_grad, 'fsdp', scatter_dimension=1, tiled=True)  47.2 us
    reduce_scatter x1, waiting for transfers between devices, on_device(): lax.psum_scatter(up_grad, 'fsdp', scatter_dimension=0, tiled=True)  46.9 us
    psum x1, waiting for transfers between devices, on_device(): lax.psum((spread[0], spread[1], spread[2], spread[3]), 'ctx')  42.5 us
    reduce_scatter x1, waiting for transfers between devices, on_device(): lax.psum_scatter(qkv_grad, 'fsdp', scatter_dimension=0, tiled=True)  40.7 us
  transfers between devices with their start and end apart: 15, of which 14 were waited for; matrix products, arithmetic and copies ran while one was open for 11% of the time, Pallas kernels for 0%

commit v1 on v0

--- a/solution.py
+++ b/solution.py
@@ -1,3 +1,4 @@
+import functools
 import jax
 import jax.numpy as jnp
 from jax import lax
@@ -7,6 +8,13 @@
 EPSILON = 1e-06
 
 
+def close_forms(x_in, axis_id):
+    return jnp.sum(lax.all_gather(x_in, axis_id), axis=0)
+
+
+take_limits = functools.partial(close_forms, axis_id="tp")
+
+
 def layer_norm(values, gain, shift):
     center = values - jnp.mean(values, axis=-1, keepdims=True)
     spread = jnp.mean(center * center, axis=-1, keepdims=True)
@@ -18,7 +26,7 @@
 
 
 def head_total(partial_sum):
-    return lax.psum(partial_sum, "tp")
+    return take_limits(partial_sum)
 
 
 def attend(queries, keys_all, values_all, key_keep, scale_factor):

time: 1300 us -> 2010 us (1.55)
  waiting for transfers between devices: 1010 us -> 1640 us
  other arithmetic: 71.5 us -> 142 us
    all_gather x0 -> x4, waiting for transfers between devices: none -> 1360 us  [close_forms(): return jnp.sum(lax.all_gather(x_in, axis_id), axis=0)]
    psum x3 -> x0, waiting for transfers between devices: 731 us -> none  [head_total(): return lax.psum(partial_sum, 'tp')]
    reduce_sum x1 -> x4, other arithmetic: 2.32 us -> 46.4 us  [close_forms(): return jnp.sum(lax.all_gather(x_in, axis_id), axis=0)]
    reduce_scatter x1, waiting for transfers between devices: 47.2 us -> 18 us  [on_device(): lax.psum_scatter(down_grad, 'fsdp', scatter_dimension=1, tiled=True)]
    reduce_scatter x1, waiting for transfers between devices: 2.59 us -> 28 us  [on_device(): lax.psum_scatter(out_grad, 'fsdp', scatter_dimension=1, tiled=True)]
  transfers between devices with their start and end apart: 15 -> 16, of which waited for: 14 -> 15; matrix products, arithmetic and copies ran while one was open for 11% -> 10% of each run, Pallas kernels for 0% -> 0%
where the time goes in v1:
time: 2010 us; the launch traced here: 2000 us
  waiting for transfers between devices  1640 us (82%)
  other arithmetic  142 us (7%)
  matrix products  110 us (5%)
  local copies, waits for them, and re-layouts  54 us (3%)
  blocking collectives  33 us (2%)
    all_gather x4, waiting for transfers between devices, close_forms(): return jnp.sum(lax.all_gather(x_in, axis_id), axis=0)  1360 us
    reduce_scatter x1, waiting for transfers between devices, on_device(): lax.psum_scatter(up_grad, 'fsdp', scatter_dimension=0, tiled=True)  47.2 us
    psum x1, waiting for transfers between devices, on_device(): lax.psum((spread[0], spread[1], spread[2], spread[3]), 'ctx')  46.5 us
    reduce_sum x4, other arithmetic, close_forms(): return jnp.sum(lax.all_gather(x_in, axis_id), axis=0)  46.4 us
    reduce_scatter x1, waiting for transfers between devices, on_device(): lax.psum_scatter(qkv_grad, 'fsdp', scatter_dimension=0, tiled=True)  40.4 us
  transfers between devices with their start and end apart: 16, of which 15 were waited for; matrix products, arithmetic and copies ran while one was open for 10% of the time, Pallas kernels for 0%

profile of v1, /device:TPU:0, one launch (start us, length us, event | category | flops | bytes accessed | tf_op | source)
XLA Modules:
  0.0 2000.8 jit_solution(4406925769418027453)
XLA Ops:
  16.7 15.9 all-gather.14.cloned.1.call-done
  39.5 7.6 all_gather.45
  52.5 11.3 all-gather.18.cloned.1.call-done
  75.6 14.6 all-gather.16.cloned.1.call-done
  115.2 348.0 %all-gather.24.cloned.1.call-done = f32[5120,1024]{1,0:T(8,128)} async-done(((f32[1280,1024]{1,0:T(8,128)}), f32[5120,1024]{1,0:T(8,128)}) %all-gather.24.cloned.1.call-update) | async-done | bytes 20971536 | tf_op jit(solution)/shard_map/all_gather | solution.py:12
  463.2 11.3 reduce_sum.243
  487.9 7.6 fusion.40
  495.5 15.7 all-gather.22.cloned.1.call-done
  511.2 18.4 convert_reduce_fusion.1
  548.0 344.7 %all-gather.28.cloned.1.call-done = f32[5120,1024]{1,0:T(8,128)} async-done(((f32[1280,1024]{1,0:T(8,128)}), f32[5120,1024]{1,0:T(8,128)}) %all-gather.28.cloned.1.call-update) | async-done | bytes 20971536 | tf_op jit(solution)/shard_map/all_gather | solution.py:12
  892.8 12.5 reduce_sum.249
  911.3 338.5 %all-gather.26.cloned.1.call-done = f32[5120,1024]{1,0:T(8,128)} async-done(((f32[1280,1024]{1,0:T(8,128)}), f32[5120,1024]{1,0:T(8,128)}) %all-gather.26.cloned.1.call-update) | async-done | bytes 20971536 | tf_op jit(solution)/shard_map/all_gather | solution.py:12
  1249.8 11.0 reduce_sum.247
  1260.8 9.4 fusion.35
  1282.3 7.2 fusion.13
  1293.3 7.3 multiply_reduce_fusion
  1330.9 38.3 %reduce-scatter.7.cloned.1.call-done = f32[8,160,256]{2,0,1:T(8,128)} async-done(((f32[8,320,256]{2,0,1:T(8,128)}), f32[8,160,256]{2,0,1:T(8,128)}) %reduce-scatter.7.cloned.1.call-update) | async-done | bytes 1310736 | tf_op jit(solution)/shard_map/reduce_scatter | solution.py:172
  1371.5 6.2 convolution_bitcast_fusion
  1378.2 7.7 fusion.45
  1386.0 8.7 fusion.44
  1394.8 7.5 fusion.30
  1402.6 332.2 %all-gather.30.cloned.1.call-done = f32[5120,1024]{1,0:T(8,128)} async-done(((f32[1280,1024]{1,0:T(8,128)}), f32[5120,1024]{1,0:T(8,128)}) %all-gather.30.cloned.1.call-update) | async-done | bytes 20971536 | tf_op jit(solution)/shard_map/all_gather | solution.py:12
  1734.8 11.5 reduce_sum.255
  1753.2 7.2 convert_reduce_fusion.2
  1762.3 18.0 reduce-scatter.17.cloned.1.call-done
  1780.3 47.2 %reduce-scatter.15.cloned.1.call-done = f32[256,1024]{1,0:T(8,128)} async-done(((f32[1024,1024]{1,0:T(8,128)}), f32[256,1024]{1,0:T(8,128)}) %reduce-scatter.15.cloned.1.call-update) | async-done | bytes 1048592 | tf_op jit(solution)/shard_map/reduce_scatter | solution.py:205
  1827.5 40.4 %reduce-scatter.11.cloned.1.call-done = f32[256,3,256]{2,0,1:T(8,128)} async-done(((f32[1024,3,256]{2,0,1:T(8,128)}), f32[256,3,256]{2,0,1:T(8,128)}) %reduce-scatter.11.cloned.1.call-update) | async-done | bytes 786448 | tf_op jit(solution)/shard_map/reduce_scatter | solution.py:203
  1867.9 28.0 %reduce-scatter.13.cloned.1.call-done = f32[256,256]{1,0:T(8,128)} async-done(((f32[256,1024]{1,0:T(8,128)}), f32[256,256]{1,0:T(8,128)}) %reduce-scatter.13.cloned.1.call-update) | async-done | bytes 262160 | tf_op jit(solution)/shard_map/reduce_scatter | solution.py:204
  1895.9 8.2 reduce_sum.266
  1905.8 8.2 reduce_sum.264
  1913.9 25.3 %all-reduce = (f32[2,256]{1,0:T(2,128)}, f32[1024]{0:T(1024)}, f32[1024]{0:T(1024)}, f32[1024]{0:T(1024)}, f32[1024]{0:T(1024)}, /*index=5*/f32[1024]{0:T(1024)}, f32[1024]{0:T(1024)}, f32[1024]{0:T(1024)}) all-reduce(f32[2,256]{1,0:T(2,128)S(1)} %convert_reduce_fusion.4, ...), channel_id=1, replica_groups=mesh['fsdp'=4,'ctx'=2,'tp'=4] {'fsdp','ctx'}, use_global_device_ids=true, to_apply=%region_20.21 | all-reduce | flops 7680 | bytes 61440 | tf_op jit(solution)/shard_map/psum | solution.py:211
  1939.3 46.5 %all-reduce.4.cloned.1.call-done = (f32[256,3,256]{2,0,1:T(8,128)}, f32[256,256]{1,0:T(8,128)}, f32[256,1024]{1,0:T(8,128)}, f32[1024,256]{1,0:T(8,128)}) async-done(((f32[256,3,256]{2,0,1:T(8,128)}, f32[256,256]{1,0:T(8,128)}, f32[256,1024]{1,0:T(8,128)}, f32[1024,256]{1,0:T(8,128)}), (f32[256,3,256]{2,0,1:T(8,128)}, f32[256,256]{1,0:T(8,128)}, f32[256,1024]{1,0:T(8,128)}, ...) | async-done | bytes 3145744 | tf_op jit(solution)/shard_map/psum | solution.py:208
  (182 shorter events, 163.9 us)
Async XLA Ops:
  7.2 25.4 %all-gather.14.cloned.1.call-start = ((), (), s32[]{:S(2)}) async-start(), calls=%async_computation.6 | async-start | bytes 1966080 | tf_op jit(solution)/shard_map/all_gather | solution.py:112
  9.3 54.5 %all-gather.18.cloned.1.call-start = ((), (), s32[]{:S(2)}) async-start(), calls=%async_computation.8 | async-start | bytes 1966080 | tf_op jit(solution)/shard_map/all_gather | solution.py:131
  11.6 20.9 %copy-start.24 = (f32[1280]{0:T(1024)}, f32[1280]{0:T(1024)S(1)}, u32[]{:S(2)}) copy-start(f32[1280]{0:T(1024)S(1)} %div.57) | copy-start | bytes 15364
  11.7 20.9 %copy-start.20 = (f32[1024]{0:T(1024)S(1)}, f32[1024]{0:T(1024)}, u32[]{:S(2)}) copy-start(f32[1024]{0:T(1024)} %param.26) | copy-start | bytes 12292
  11.7 20.9 %copy-start.34 = (f32[1024]{0:T(1024)S(1)}, f32[1024]{0:T(1024)}, u32[]{:S(2)}) copy-start(f32[1024]{0:T(1024)} %param.27) | copy-start | bytes 12292
  13.1 19.4 copy-start.15
  13.2 19.3 copy-start.26
  16.7 22.8 %copy-start.14 = (f32[256,256]{1,0:T(8,128)S(1)}, f32[256,256]{1,0:T(8,128)}, u32[]{:S(2)}) copy-start(f32[256,256]{1,0:T(8,128)} %param.20) | copy-start | bytes 786436
  38.2 9.3 copy-start.23
  39.4 50.8 %all-gather.16.cloned.1.call-start = ((), (), s32[]{:S(2)}) async-start(), calls=%async_computation.7 | async-start | bytes 1966080 | tf_op jit(solution)/shard_map/all_gather | solution.py:132
  47.1 416.1 %all-gather.24.cloned.1.call-start = ((), (), s32[]{:S(2)}) async-start(), calls=%async_computation.17 | async-start | bytes 26214400 | tf_op jit(solution)/shard_map/all_gather | solution.py:12
  106.2 381.7 %all-gather.20.cloned.1.call-start = ((), (), s32[]{:S(2)}) async-start(), calls=%async_computation.9 | async-start | bytes 2621440 | tf_op jit(solution)/shard_map/all_gather | solution.py:114
  108.4 402.9 %all-gather.22.cloned.1.call-start = ((), (), s32[]{:S(2)}) async-start(), calls=%async_computation.10 | async-start | bytes 2621440 | tf_op jit(solution)/shard_map/all_gather | solution.py:115
  110.5 782.2 %all-gather.28.cloned.1.call-start = ((), (), s32[]{:S(2)}) async-start(), calls=%async_computation.19 | async-start | bytes 26214400 | tf_op jit(solution)/shard_map/all_gather | solution.py:12
  463.2 11.3 copy-start.22
  487.9 23.3 %copy-start.29 = (f32[1024]{0:T(1024)S(1)}, f32[1024]{0:T(1024)}, u32[]{:S(2)}) copy-start(f32[1024]{0:T(1024)} %param.23) | copy-start | bytes 12292
  511.2 19.8 copy-start.33
  535.8 714.0 %all-gather.26.cloned.1.call-start = ((), (), s32[]{:S(2)}) async-start(), calls=%async_computation.18 | async-start | bytes 26214400 | tf_op jit(solution)/shard_map/all_gather | solution.py:12
  548.0 781.4 %reduce-scatter.9.cloned.1.call-start = ((), (), s32[]{:S(2)}) async-start(), calls=%async_computation.12 | async-start | bytes 3932160 | tf_op jit(solution)/shard_map/reduce_scatter | solution.py:178
  1249.8 11.0 copy-start.30
  1293.0 76.1 %reduce-scatter.7.cloned.1.call-start = ((), (), s32[]{:S(2)}) async-start(), calls=%async_computation.11 | async-start | bytes 3932160 | tf_op jit(solution)/shard_map/reduce_scatter | solution.py:172
  1312.6 422.1 %all-gather.30.cloned.1.call-start = ((), (), s32[]{:S(2)}) async-start(), calls=%async_computation.20 | async-start | bytes 26214400 | tf_op jit(solution)/shard_map/all_gather | solution.py:12
  1377.8 402.5 %reduce-scatter.17.cloned.1.call-start = ((), (), s32[]{:S(2)}) async-start(), calls=%async_computation.16 | async-start | bytes 5242880 | tf_op jit(solution)/shard_map/reduce_scatter | solution.py:206
  1385.9 8.9 copy-start.21
  1385.9 8.9 copy-start.25
  1385.9 8.9 copy-start.27
  1386.0 8.9 copy-start.35
  1386.0 441.5 %reduce-scatter.15.cloned.1.call-start = ((), (), s32[]{:S(2)}) async-start(), calls=%async_computation.15 | async-start | bytes 5242880 | tf_op jit(solution)/shard_map/reduce_scatter | solution.py:205
  1394.7 473.2 %reduce-scatter.11.cloned.1.call-start = ((), (), s32[]{:S(2)}) async-start(), calls=%async_computation.13 | async-start | bytes 3932160 | tf_op jit(solution)/shard_map/reduce_scatter | solution.py:203
  1402.4 493.5 %reduce-scatter.13.cloned.1.call-start = ((), (), s32[]{:S(2)}) async-start(), calls=%async_computation.14 | async-start | bytes 1310720 | tf_op jit(solution)/shard_map/reduce_scatter | solution.py:204
  1734.8 11.5 copy-start.13
  1762.3 223.5 %all-reduce.4.cloned.1.call-start = ((), (), s32[]{:S(2)}) async-start(), calls=%async_computation.21 | async-start | bytes 6291456 | tf_op jit(solution)/shard_map/psum | solution.py:208
  (21 other events, 85.9 us)
Sparse Core Ops, SparseCore 0:
  10.2 22.3 all-gather.13
  39.5 24.2 all-gather.17
  65.9 24.2 all-gather.15
  106.3 356.8 all-gather.23
  465.2 21.1 all-gather.19
  488.4 22.8 all-gather.21
  535.9 356.8 all-gather.27
  894.4 355.4 all-gather.25
  1293.2 36.1 reduce-scatter.8
  1331.5 37.5 reduce-scatter.6
  1377.9 356.8 all-gather.29
  1737.1 43.0 reduce-scatter.16
  1783.0 44.4 reduce-scatter.14
  1829.9 37.9 reduce-scatter.10
  1871.0 24.8 reduce-scatter.12
  1898.2 87.5 all-reduce.3
